TPU v7x, 32 devices: a whole 2x2x4 slice. The times are simulated.
32 devices in a mesh: freq: 4 (over z), chan: 8 (over y, x, core).
Axes of the slice: x: 2, y: 2, z: 4, core: 2. Of those that a mesh axis runs over, the one named last changes fastest.
Arguments:
- raw_strain: bfloat16 [8, 32, 150000], P('chan', 'freq'), may hold values from -6 to 6
- fir_taps: bfloat16 [20], replicated, may hold values from -1.25 to 1.25
- band_bins: int32 [240], replicated, may hold values from 60 to 359, as said below
- live_mask: int32 [8, 32], P('chan', 'freq'), may hold values 0 or 1
Outputs:
- cross_spectra: float32 [240, 2, 256, 256], P('freq', None, 'chan')
Inputs may be any that keep to these rules, and one draw needn't show every extreme that they name: `band_bins`: strictly increasing; the first is 60 and the last is 359.
All inputs are finite; a program needn't handle non-finite values. No bound on the sum of `live_mask` on one device may be relied on, other than what follows from the above.
Results may differ from a plain program's by a relative error of at most 0.0067.
Values may be sent and summed in bfloat16 or wider, within the bound.
No kernel may reach another device: no remote copies, remote signals or barrier semaphores. Data moves between devices by JAX's collectives and lax.ppermute only.
A program may use at most 64 MiB of HBM per device.

v0:
```python
import math
import jax
import jax.numpy as jnp
from jax import lax
from jax.sharding import PartitionSpec as P

WIN = 10
DECIM = 10
NT = 1500


def make_table(band_bins, length):
    times = jnp.arange(length, dtype=jnp.int32)[:, None]
    phase = times * band_bins[None, :] % length
    angle = phase.astype(jnp.float32) * jnp.float32(2.0 * math.pi / length)
    return jnp.concatenate([jnp.cos(angle), -jnp.sin(angle)], axis=1).astype(jnp.bfloat16)


def correlate(rows_spec, cols_spec, windows):
    bins = rows_spec.shape[0]
    height = rows_spec.shape[3]
    width = cols_spec.shape[3]
    real_left = rows_spec.reshape(bins, 2 * windows, height)
    imag_left = jnp.concatenate([rows_spec[:, 1], -rows_spec[:, 0]], axis=1)
    left_both = jnp.stack([real_left, imag_left], axis=1)
    right_side = cols_spec.reshape(bins, 2 * windows, width)
    prod = jnp.einsum("fski,fkj->fsij", left_both, right_side, preferred_element_type=jnp.float32)
    return prod / windows


def decimate(raw_strain, fir_taps, rows, windows, length, factor):
    outputs = length // 10
    span = outputs * factor
    blocks = raw_strain.reshape(rows * windows * 10, span)
    taps_float = fir_taps.astype(jnp.float32)
    tap_count = fir_taps.shape[0]
    sample_idx = jnp.arange(span, dtype=jnp.int32)[:, None]
    out_idx = jnp.arange(outputs, dtype=jnp.int32)[None, :]
    tap_idx = factor * out_idx + factor - 1 - sample_idx
    valid = (tap_idx >= 0) & (tap_idx < tap_count)
    band = jnp.where(valid, taps_float[jnp.clip(tap_idx, 0, tap_count - 1)], 0.0).astype(
        jnp.bfloat16
    )
    current = jnp.dot(blocks, band, preferred_element_type=jnp.float32)
    tail = blocks[:, span - factor :]
    tail_taps = taps_float[2 * factor - 1 - jnp.arange(factor, dtype=jnp.int32)].astype(
        jnp.bfloat16
    )
    carried = jnp.dot(tail, tail_taps[:, None], preferred_element_type=jnp.float32)
    carried = carried.reshape(rows * windows, 10)
    carried = jnp.pad(carried, ((0, 0), (1, 0)))[:, :10]
    current = current.reshape(rows * windows, 10, outputs)
    current = current.at[:, :, 0].add(carried)
    return current.reshape(rows, windows, length).astype(jnp.bfloat16)


def shards(raw_strain, fir_taps, band_bins, live_mask):
    rows = raw_strain.shape[1]
    windows = WIN
    length = NT
    factor = DECIM
    bins = band_bins.shape[0]
    table = make_table(band_bins, length)
    decimated = decimate(raw_strain, fir_taps, rows, windows, length, factor)
    spectrum = jnp.dot(
        decimated.reshape(rows * windows, length), table, preferred_element_type=jnp.float32
    )
    spectrum = spectrum.reshape(rows, windows, 2, bins)
    power = jnp.sum(spectrum * spectrum, axis=(2, 3)) / bins
    scale = lax.rsqrt(power + 1e-06) * live_mask[0].astype(jnp.float32)[:, None]
    whitened = (spectrum * scale[:, :, None, None]).astype(jnp.bfloat16)
    ordered = jnp.transpose(whitened, (3, 2, 1, 0))
    own = lax.all_to_all(ordered, "freq", split_axis=0, concat_axis=3, tiled=True)
    return correlate(own, lax.all_gather(own, "chan", axis=3, tiled=True), windows)


def solution(mesh):
    in_specs = (P("chan", "freq", None), P(), P(), P("chan", "freq"))
    out_specs = P("freq", None, "chan", None)
    return jax.shard_map(shards, mesh=mesh, in_specs=in_specs, out_specs=out_specs, check_vma=False)
```

profile of v0, /device:TPU:0, one launch (start us, length us, event | category | flops | bytes accessed | tf_op | source)
XLA Modules:
  0.0 82.6 jit_solution(9209558224427891211)
XLA Ops:
  0.0 2.1 %fusion.129 = (bf16[1]{0:T(256)(128)(2,1)}, bf16[1]{0:T(256)(128)(2,1)}, bf16[1]{0:T(256)(128)(2,1)}, bf16[1]{0:T(256)(128)(2,1)}, bf16[1]{0:T(256)(128)(2,1)}, ...) fusion(bf16[20]{0:T(256)(128)(2,1)} %param.7), kind=kLoop, calls=%fused_computation.157 | loop fusion | bytes 76 | tf_op jit(solution)/shard_map/gather | solution.py:41
  2.1 1.2 %slice.57 = bf16[1]{0:T(256)(128)(2,1)} slice(bf16[20]{0:T(256)(128)(2,1)} %param.7), slice={[17:18]} | slice | bytes 4 | tf_op jit(solution)/shard_map/gather | solution.py:41
  3.3 4.8 %reshape.254 = bf16[1200000]{0:T(1024)(128)(2,1)S(1)} reshape(bf16[1,8,150000]{2,1,0:T(8,128)(2,1)} %param.6) | data formatting | bytes 4800000
  8.1 5.1 %reshape.153 = bf16[800,1500]{1,0:T(8,128)(2,1)} reshape(bf16[1200000]{0:T(1024)(128)(2,1)S(1)} %reshape.254) | data formatting | bytes 4800000 | tf_op jit(solution)/shard_map/reshape | solution.py:34
  13.3 1.0 %slice.63 = bf16[800,10]{1,0:T(8,128)(2,1)S(1)} slice(bf16[800,1500]{1,0:T(8,128)(2,1)} %reshape.153), slice={[0:800], [1490:1500]} | slice | bytes 32000 | tf_op jit(solution)/shard_map/slice | solution.py:45
  14.3 17.4 %convolution_bitcast_fusion = f32[800,150]{0,1:T(8,128)S(1)} fusion(bf16[800,1500]{1,0:T(8,128)(2,1)} %reshape.153, bf16[]{:T(256)} %bitcast.27, bf16[]{:T(256)} %bitcast.28, bf16[]{:T(256)} %bitcast.29, bf16[]{:T(256)} %bitcast.30, bf16[]{:T(256)} %bitcast.31, bf16[]{:T(256)} %bitcast.33, bf16[]{:T(256)} %bitcast.32, bf16[]{:T(256)} %bitcast.2, ...), kind=kOutput, calls=%fused_computation.64 | convolution fusion | flops 370800000 | bytes 2880640 | tf_op jit(solution)/shard_map/dot_general | solution.py:44
  31.7 0.3 copy.30
  32.1 0.1 copy.52
  32.3 0.2 dot_general.24
  32.6 0.7 gather_fusion
  33.5 0.4 copy.32
  34.0 5.3 %scatter-add.4 = f32[80,10,150]{2,1,0:T(8,128)S(1)} dynamic-update-slice(f32[80,10,150]{2,1,0:T(8,128)S(1)} %reshape.154, f32[80,10,1]{2,1,0:T(8,128)S(1)} %slice_add_fusion, s32[]{:T(128)} %constant.58.clone.1, s32[]{:T(128)} %constant.58.clone.1, s32[]{:T(128)} %constant.58.clone.1) | dynamic-update-slice | bytes 6404 | tf_op jit(solution)/shard_map/scatter-add | solution.py:53
  39.4 0.7 reshape.250
  40.1 6.6 %cosine_convert_fusion = (bf16[1500,240]{0,1:T(8,128)(2,1)S(1)}, bf16[1500,240]{0,1:T(8,128)(2,1)S(1)}) fusion(s32[240]{0:T(256)S(1)} %copy-done.1), kind=kLoop, calls=%fused_computation.59 | loop fusion | flops 4320000 | bytes 1440960 | tf_op jit(solution)/shard_map/convert
  46.8 0.7 multiply_reduce_fusion.1
  47.7 1.3 %copy.33 = bf16[240,2,10,8]{2,1,3,0:T(2,128)(2,1)S(1)} copy(bf16[240,2,10,8]{0,2,1,3:T(8,128)(2,1)S(1)} %fusion.103) | data formatting | bytes 153600 | tf_op jit(solution)/shard_map/convert_element_type | solution.py:71
  49.0 1.6 %reshape.256 = bf16[4,2,4800]{2,1,0:T(2,128)(2,1)S(1)} reshape(bf16[240,8,2,10]{3,2,1,0:T(2,128)(2,1)S(1)} %bitcast.166) | data formatting | bytes 153600
  50.5 11.9 %all_to_all.18 = bf16[4,2,4800]{2,1,0:T(2,128)(2,1)S(1)} all-to-all(bf16[4,2,4800]{2,1,0:T(2,128)(2,1)S(1)} %reshape.256), channel_id=1, replica_groups=mesh['freq'=4,'chan'=8] {'freq'}, dimensions={0} | all-to-all | bytes 153600 | tf_op jit(solution)/shard_map/all_to_all | solution.py:73
  62.4 2.3 %reshape.257 = bf16[240,8,2,10]{3,2,1,0:T(2,128)(2,1)S(1)} reshape(bf16[4,2,4800]{2,1,0:T(2,128)(2,1)S(1)} %all_to_all.18) | data formatting | bytes 153600
  64.8 1.3 %copy.47 = bf16[4,60,2,10,8]{1,0,4,3,2:T(4,128)(2,1)S(1)} copy(bf16[4,60,2,10,8]{3,2,4,1,0:T(2,128)(2,1)S(1)} %bitcast.167) | data formatting | bytes 153600 | tf_op jit(solution)/shard_map/all_to_all | solution.py:73
  66.1 12.1 %all_gather.3 = bf16[60,2,10,256]{0,3,2,1:T(8,128)(2,1)S(1)} all-gather(bf16[60,2,10,32]{0,3,2,1:T(8,128)(2,1)S(1)} %bitcast.168), channel_id=1, replica_groups=mesh['freq'=4,'chan'=8] {'chan'}, dimensions={3}, use_global_device_ids=true | all-gather | bytes 691200 | tf_op jit(solution)/shard_map/all_gather | solution.py:74
  78.3 0.9 %copy.46 = bf16[60,20,256,1]{2,1,3,0:T(8,128)(2,1)S(1)} copy(bf16[60,20,256,1]{0,2,1,3:T(8,128)(2,1)S(1)} %bitcast.165) | data formatting | bytes 1228800 | tf_op jit(solution)/shard_map/reshape | solution.py:26
  79.3 0.6 copy.38
  79.9 2.7 %convolution_multiply_fusion = f32[60,2,32,256]{3,2,1,0:T(8,128)} fusion(bf16[60,2,20,32]{3,2,1,0:T(8,128)(2,1)S(1)} %copy.38, bf16[60,20,256,1]{2,1,3,0:T(8,128)(2,1)S(1)} %copy.46), kind=kOutput, calls=%fused_computation.3 | convolution fusion | flops 40304640 | bytes 4700160 | tf_op jit(solution)/shard_map/fski,fkj->fsij/dot_general | solution.py:27
  (24 shorter events, 1.1 us)
Async XLA Ops:
  32.0 0.7 copy-start
  39.3 0.8 copy-start.1
  39.4 7.3 %copy-start.2 = (s32[1,8]{1,0:T(1,128)S(1)}, s32[1,8]{1,0:T(1,128)}, u32[]{:S(2)}) copy-start(s32[1,8]{1,0:T(1,128)} %param.9) | copy-start | bytes 100
where the time goes:
time: 83.1 us; the launch traced here: 82.6 us
  local copies, waits for them, and re-layouts  30.3 us (36%)
  blocking collectives  24 us (29%)
  matrix products  20.8 us (25%)
  other arithmetic  7.29 us (9%)
    dot_general x1, matrix products, decimate(): current = jnp.dot(blocks, band, preferred_element_type=jnp.float32)  17.4 us
    all_gather x1, blocking collectives, shards(): lax.all_gather(own, 'chan', axis=3, tiled=True)  12.1 us
    all_to_all x1, blocking collectives, shards(): lax.all_to_all(ordered, 'freq', split_axis=0, concat_axis=3, tiled=True)  11.9 us
    unnamed x10, local copies, waits for them, and re-layouts  8.94 us
    another operation x1, other arithmetic  6.55 us
    scatter-add x1, local copies, waits for them, and re-layouts, decimate(): current = current.at[:, :, 0].add(carried)  5.28 us
    reshape x1, local copies, waits for them, and re-layouts, decimate(): blocks = raw_strain.reshape(rows * windows * 10, span)  5.14 us
    gather x2, local copies, waits for them, and re-layouts, decimate(): taps_float[jnp.clip(tap_idx, 0, tap_count - 1)]  3.32 us

commit v1 on v0

--- a/solution.py
+++ b/solution.py
@@ -70,7 +70,10 @@
     scale = lax.rsqrt(power + 1e-06) * live_mask[0].astype(jnp.float32)[:, None]
     whitened = (spectrum * scale[:, :, None, None]).astype(jnp.bfloat16)
     ordered = jnp.transpose(whitened, (3, 2, 1, 0))
-    own = lax.all_to_all(ordered, "freq", split_axis=0, concat_axis=3, tiled=True)
+    own = jnp.concatenate(
+        lax.all_to_all(jnp.stack(jnp.split(ordered, lax.axis_size("freq"), axis=0)), "freq", 0, 0),
+        axis=3,
+    )
     return correlate(own, lax.all_gather(own, "chan", axis=3, tiled=True), windows)
 
 

time: 83.1 us -> 78.1 us (0.940)
  local copies, waits for them, and re-layouts: 30.3 us -> 25 us
    unnamed x10, local copies, waits for them, and re-layouts: 8.94 us -> 5.61 us
    all_to_all x2 -> x1, local copies, waits for them, and re-layouts: 1.36 us -> 0.04 us  [shards(): lax.all_to_all(jnp.stack(jnp.split(ordered, lax.axis_size('freq'), axis=0...]
    convert_element_type x1 -> x0, local copies, waits for them, and re-layouts: 1.26 us -> none  [shards(): whitened = (spectrum * scale[:, :, None, None]).astype(jnp.bfloat16)]
    all_gather x0 -> x1, local copies, waits for them, and re-layouts: none -> 1.15 us  [shards(): lax.all_gather(own, 'chan', axis=3, tiled=True)]
    another operation x1 -> x2, other arithmetic: 6.55 us -> 6.63 us
where the time goes in v1:
time: 78.1 us; the launch traced here: 77.6 us
  local copies, waits for them, and re-layouts  25 us (32%)
  blocking collectives  24 us (31%)
  matrix products  20.9 us (27%)
  other arithmetic  7.37 us (9%)
    dot_general x1, matrix products, decimate(): current = jnp.dot(blocks, band, preferred_element_type=jnp.float32)  17.4 us
    all_gather x1, blocking collectives, shards(): lax.all_gather(own, 'chan', axis=3, tiled=True)  12.1 us
    all_to_all x1, blocking collectives, shards(): lax.all_to_all(jnp.stack(jnp.split(ordered, lax.axis_size('freq'), axis=0...  11.9 us
    another operation x1, other arithmetic  6.55 us
    unnamed x10, local copies, waits for them, and re-layouts  5.61 us
    scatter-add x1, local copies, waits for them, and re-layouts, decimate(): current = current.at[:, :, 0].add(carried)  5.28 us
    reshape x1, local copies, waits for them, and re-layouts, decimate(): blocks = raw_strain.reshape(rows * windows * 10, span)  5.14 us
    gather x2, local copies, waits for them, and re-layouts, decimate(): taps_float[jnp.clip(tap_idx, 0, tap_count - 1)]  3.33 us

profile of v1, /device:TPU:0, one launch (start us, length us, event | category | flops | bytes accessed | tf_op | source)
XLA Modules:
  0.0 77.6 jit_solution(2513810363816606618)
XLA Ops:
  0.0 2.1 %fusion.130 = (bf16[1]{0:T(256)(128)(2,1)}, bf16[1]{0:T(256)(128)(2,1)}, bf16[1]{0:T(256)(128)(2,1)}, bf16[1]{0:T(256)(128)(2,1)}, bf16[1]{0:T(256)(128)(2,1)}, ...) fusion(bf16[20]{0:T(256)(128)(2,1)} %param.7), kind=kLoop, calls=%fused_computation.163 | loop fusion | bytes 76 | tf_op jit(solution)/shard_map/gather | solution.py:41
  2.1 1.3 %slice.57 = bf16[1]{0:T(256)(128)(2,1)} slice(bf16[20]{0:T(256)(128)(2,1)} %param.7), slice={[17:18]} | slice | bytes 4 | tf_op jit(solution)/shard_map/gather | solution.py:41
  3.3 4.8 %reshape.261 = bf16[1200000]{0:T(1024)(128)(2,1)S(1)} reshape(bf16[1,8,150000]{2,1,0:T(8,128)(2,1)} %param.6) | data formatting | bytes 4800000
  8.1 5.1 %reshape.158 = bf16[800,1500]{1,0:T(8,128)(2,1)} reshape(bf16[1200000]{0:T(1024)(128)(2,1)S(1)} %reshape.261) | data formatting | bytes 4800000 | tf_op jit(solution)/shard_map/reshape | solution.py:34
  13.3 1.0 %slice.63 = bf16[800,10]{1,0:T(8,128)(2,1)S(1)} slice(bf16[800,1500]{1,0:T(8,128)(2,1)} %reshape.158), slice={[0:800], [1490:1500]} | slice | bytes 32000 | tf_op jit(solution)/shard_map/slice | solution.py:45
  14.3 17.4 %convolution_bitcast_fusion = f32[800,150]{0,1:T(8,128)S(1)} fusion(bf16[800,1500]{1,0:T(8,128)(2,1)} %reshape.158, bf16[]{:T(256)} %bitcast.27, bf16[]{:T(256)} %bitcast.28, bf16[]{:T(256)} %bitcast.29, bf16[]{:T(256)} %bitcast.30, bf16[]{:T(256)} %bitcast.31, bf16[]{:T(256)} %bitcast.33, bf16[]{:T(256)} %bitcast.32, bf16[]{:T(256)} %bitcast.2, ...), kind=kOutput, calls=%fused_computation.64 | convolution fusion | flops 370800000 | bytes 2880640 | tf_op jit(solution)/shard_map/dot_general | solution.py:44
  31.7 0.3 copy.27
  32.1 0.1 copy.45
  32.3 0.2 dot_general.24
  32.6 0.7 gather_fusion
  33.3 0.1 multiply_reduce_fusion
  33.5 0.4 copy.29
  34.0 5.3 %scatter-add.4 = f32[80,10,150]{2,1,0:T(8,128)S(1)} dynamic-update-slice(f32[80,10,150]{2,1,0:T(8,128)S(1)} %reshape.159, f32[80,10,1]{2,1,0:T(8,128)S(1)} %slice_add_fusion, s32[]{:T(128)} %constant.58.clone.1, s32[]{:T(128)} %constant.58.clone.1, s32[]{:T(128)} %constant.58.clone.1) | dynamic-update-slice | bytes 6404 | tf_op jit(solution)/shard_map/scatter-add | solution.py:53
  39.4 0.7 reshape.257
  40.1 6.6 %cosine_convert_fusion = (bf16[1500,240]{0,1:T(8,128)(2,1)S(1)}, bf16[1500,240]{0,1:T(8,128)(2,1)S(1)}) fusion(s32[240]{0:T(256)S(1)} %copy-done.1), kind=kLoop, calls=%fused_computation.59 | loop fusion | flops 4320000 | bytes 1440960 | tf_op jit(solution)/shard_map/convert
  46.8 0.7 multiply_reduce_fusion.1
  48.0 0.3 reshape.263
  48.2 11.9 %all_to_all.5 = bf16[4,2,4800]{2,1,0:T(2,128)(2,1)S(1)} all-to-all(bf16[4,2,4800]{2,1,0:T(2,128)(2,1)S(1)} %reshape.263), channel_id=1, replica_groups=mesh['freq'=4,'chan'=8] {'freq'}, dimensions={0} | all-to-all | bytes 153600 | tf_op jit(solution)/shard_map/all_to_all | solution.py:74
  60.2 0.3 reshape.264
  60.5 0.2 copy.32
  60.7 12.1 %all_gather.3 = bf16[60,2,10,256]{0,1,2,3:T(2,128)(2,1)S(1)} all-gather(bf16[60,2,10,32]{0,1,2,3:T(2,128)(2,1)S(1)} %copy.32), channel_id=1, replica_groups=mesh['freq'=4,'chan'=8] {'chan'}, dimensions={3}, use_global_device_ids=true | all-gather | bytes 691200 | tf_op jit(solution)/shard_map/all_gather | solution.py:77
  72.8 1.1 %copy.33 = bf16[60,2,10,256]{3,0,2,1:T(8,128)(2,1)S(1)} copy(bf16[60,2,10,256]{0,1,2,3:T(2,128)(2,1)S(1)} %all_gather.3) | data formatting | bytes 1228800 | tf_op jit(solution)/shard_map/all_gather | solution.py:77
  74.1 0.6 copy.34
  74.7 2.9 %convolution_multiply_fusion = f32[60,2,32,256]{3,2,1,0:T(8,128)} fusion(bf16[60,2,20,32]{3,2,1,0:T(8,128)(2,1)S(1)} %copy.34, bf16[60,20,256,1]{2,0,1,3:T(8,128)(2,1)S(1)} %bitcast.177), kind=kOutput, calls=%fused_computation.3 | convolution fusion | flops 40304640 | bytes 4700160 | tf_op jit(solution)/shard_map/fski,fkj->fsij/dot_general | solution.py:27
  (26 shorter events, 1.3 us)
Async XLA Ops:
  32.0 0.7 copy-start
  39.3 0.8 %copy-start.1 = (s32[240]{0:T(256)S(1)}, s32[240]{0:T(256)}, u32[]{:S(2)}) copy-start(s32[240]{0:T(256)} %param.8) | copy-start | bytes 2884
  39.4 7.3 %copy-start.2 = (s32[1,8]{1,0:T(1,128)S(1)}, s32[1,8]{1,0:T(1,128)}, u32[]{:S(2)}) copy-start(s32[1,8]{1,0:T(1,128)} %param.9) | copy-start | bytes 100
